TPU v7x, 128 devices: a whole 4x4x4 slice. The times are simulated.
128 devices in a mesh: blk: 16 (over z_lo, x, core), narrow: 8 (over z_hi, y).
Axes of the slice: x: 4, y: 4, z: 4 (z_hi: 2, z_lo: 2; z = z_hi * 2 + z_lo), core: 2. Of those that a mesh axis runs over, the one named last changes fastest.
Arguments:
- codes: bfloat16 [24576, 12288], P(('blk', 'narrow')), may hold values from -24 to 24
- signals: bfloat16 [24576, 192], P(('blk', 'narrow')), may hold values from -6 to 6
- dictionary: bfloat16 [12288, 192], P('blk'), may hold values from -0.0546875 to 0.0546875
Outputs:
- new_codes: bfloat16 [24576, 12288], P(('blk', 'narrow'))
- dict_grad: float32 [12288, 192], P(('blk', 'narrow'))
All inputs are finite; a program needn't handle non-finite values.
Results may differ from a plain program's by a relative error of at most 0.0095.
Values may be sent and summed in bfloat16 or wider, within the bound.
No kernel may reach another device: no remote copies, remote signals or barrier semaphores. Data moves between devices by JAX's collectives and lax.ppermute only.
A program may use at most 64 MiB of HBM per device.

v0:
```python
import jax
import jax.numpy as jnp
from jax import lax
from jax.sharding import PartitionSpec as P


def shrink(values):
    return jnp.sign(values) * jnp.maximum(jnp.abs(values) - 0.5, 0.0)


def body(codes, signals, dictionary):
    row_count = codes.shape[0]
    blk_size = lax.axis_size("blk")
    narrow_size = lax.axis_size("narrow")
    signal_float = signals.astype(jnp.float32)
    columns = codes
    estimate = jnp.dot(
        columns,
        lax.all_gather(dictionary, "blk", axis=0, tiled=True),
        preferred_element_type=jnp.float32,
    )
    misfit = (estimate - signal_float).astype(jnp.bfloat16)
    atoms_part = lax.all_gather(dictionary, "blk", axis=0, tiled=True)
    columns = codes
    correlation = lax.dot_general(
        misfit, atoms_part, (((1,), (1,)), ((), ())), preferred_element_type=jnp.float32
    )
    fresh_cols = shrink(columns.astype(jnp.float32) - 4.0 * correlation).astype(jnp.bfloat16)
    second = jnp.dot(fresh_cols, atoms_part, preferred_element_type=jnp.float32)
    misfit_two = (second - signal_float).astype(jnp.bfloat16)
    grad_scale = float(row_count * blk_size * narrow_size) ** (-0.5)
    columns = fresh_cols
    product = lax.dot_general(
        columns, misfit_two, (((0,), (0,)), ((), ())), preferred_element_type=jnp.float32
    )
    dict_grad = lax.psum_scatter(
        product * grad_scale, ("blk", "narrow"), scatter_dimension=0, tiled=True
    )
    return (fresh_cols, dict_grad)


def solution(mesh):
    placed = (P(("blk", "narrow"), None), P(("blk", "narrow"), None), P("blk", None))
    return jax.shard_map(
        body,
        mesh=mesh,
        in_specs=placed,
        out_specs=(P(("blk", "narrow"), None), P(("blk", "narrow"), None)),
        check_vma=False,
    )
```

profile of v0, /device:TPU:0, one launch (start us, length us, event | category | flops | bytes accessed | tf_op | source)
XLA Modules:
  0.0 752.3 jit_solution(6917375865547376117)
XLA Ops:
  7.2 0.0 all-gather.2.cloned.1.call-start
  7.2 0.7 all-gather.2.cloned.1.call-update
  7.9 0.0 copy-start.1
  7.9 0.0 reduce-scatter.2.cloned.1.call-start
  8.0 42.0 %all-gather.2.cloned.1.call-done = bf16[12288,192]{0,1:T(8,128)(2,1)} async-done(((bf16[768,192]{0,1:T(8,128)(2,1)}), bf16[12288,192]{0,1:T(8,128)(2,1)}) %all-gather.2.cloned.1.call-update) | async-done | bytes 4718608 | tf_op jit(solution)/shard_map/all_gather | solution.py:19
  50.0 16.0 %multiply_convert_fusion = bf16[192,12288]{1,0:T(8,128)(2,1)} fusion(bf16[12288,192]{0,1:T(8,128)(2,1)} %all-gather.2.cloned.1.call-done, bf16[192,12288]{1,0:T(8,128)(2,1)} %param.3, bf16[192,192]{1,0:T(8,128)(2,1)} %param.4), kind=kOutput, calls=%fused_computation.3 | convolution fusion | flops 1833283584 | bytes 14229504 | tf_op jit(solution)/shard_map/dot_general | solution.py:25
  66.0 0.0 copy-done.1
  66.0 0.0 copy-start
  66.0 5.3 fusion.2
  71.3 0.0 copy-done
  71.3 6.4 convolution_multiply_fusion
  77.8 0.0 reduce-scatter.2.cloned.1.call-update
  77.8 667.7 %reduce-scatter.2.cloned.1.call-done = f32[96,192]{1,0:T(8,128)} async-done(((f32[12288,192]{1,0:T(8,128)}), f32[96,192]{1,0:T(8,128)}) %reduce-scatter.2.cloned.1.call-update) | async-done | bytes 73744 | tf_op jit(solution)/shard_map/reduce_scatter | solution.py:36
Async XLA Ops:
  7.2 42.8 %all-gather.2.cloned.1.call-start = ((), (), s32[]{:S(2)}) async-start(), calls=%async_computation.1 | async-start | bytes 5013504 | tf_op jit(solution)/shard_map/all_gather | solution.py:19
  7.9 58.1 %copy-start.1 = (bf16[192,192]{1,0:T(8,128)(2,1)S(1)}, bf16[192,192]{1,0:T(8,128)(2,1)}, u32[]{:S(2)}) copy-start(bf16[192,192]{1,0:T(8,128)(2,1)} %param.4) | copy-start | bytes 221188
  7.9 737.5 %reduce-scatter.2.cloned.1.call-start = ((), (), s32[]{:S(2)}) async-start(), calls=%async_computation.2 | async-start | bytes 12681216 | tf_op jit(solution)/shard_map/reduce_scatter | solution.py:36
  66.0 5.3 copy-start
Sparse Core Ops, SparseCore 0:
  9.6 40.2 all-gather.1
  77.9 667.4 reduce-scatter.1
where the time goes:
time: 752 us
  waiting for transfers between devices  710 us (94%)
  matrix products  27.8 us (4%)
  between operations  14.1 us (2%)
    reduce_scatter x1, waiting for transfers between devices, body(): lax.psum_scatter(product * grad_scale, ('blk', 'narrow'), scatter_dimensi...  668 us
    all_gather x1, waiting for transfers between devices, body(): lax.all_gather(dictionary, 'blk', axis=0, tiled=True)  42 us
    dot_general x1, matrix products, body(): lax.dot_general(misfit, atoms_part, (((1,), (1,)), ((), ())), preferred_e...  16 us
  transfers between devices with their start and end apart: 2, of which 2 were waited for; matrix products, arithmetic and copies ran while one was open for 0% of the time, Pallas kernels for 0%

commit v1 on v0

--- a/solution.py
+++ b/solution.py
@@ -16,7 +16,9 @@
     columns = codes
     estimate = jnp.dot(
         columns,
-        lax.all_gather(dictionary, "blk", axis=0, tiled=True),
+        jnp.concatenate(
+            lax.all_to_all(jnp.stack([dictionary] * lax.axis_size("blk")), "blk", 0, 0), axis=0
+        ),
         preferred_element_type=jnp.float32,
     )
     misfit = (estimate - signal_float).astype(jnp.bfloat16)

time: 752 us -> 798 us (1.061)
  blocking collectives: 0 us -> 79.5 us
  waiting for transfers between devices: 710 us -> 672 us
    all_to_all x0 -> x1, blocking collectives: none -> 79.5 us  [body(): lax.all_to_all(jnp.stack([dictionary] * lax.axis_size('blk')), 'blk', 0, 0)]
    all_gather x1, waiting for transfers between devices: 42 us -> 1.42 us  [body(): atoms_part = lax.all_gather(dictionary, 'blk', axis=0, tiled=True)]
  transfers between devices with their start and end apart: 2 -> 2, of which waited for: 2 -> 2; matrix products, arithmetic and copies ran while one was open for 0% -> 1% of each run, Pallas kernels for 0% -> 0%
where the time goes in v1:
time: 798 us; the launch traced here: 797 us
  waiting for transfers between devices  672 us (84%)
  blocking collectives  79.5 us (10%)
  matrix products  27.8 us (3%)
  between operations  14.1 us (2%)
    reduce_scatter x1, waiting for transfers between devices, body(): lax.psum_scatter(product * grad_scale, ('blk', 'narrow'), scatter_dimensi...  670 us
    all_to_all x1, blocking collectives, body(): lax.all_to_all(jnp.stack([dictionary] * lax.axis_size('blk')), 'blk', 0, 0)  79.5 us
    dot_general x1, matrix products, body(): lax.dot_general(misfit, atoms_part, (((1,), (1,)), ((), ())), preferred_e...  16 us
  transfers between devices with their start and end apart: 2, of which 2 were waited for; matrix products, arithmetic and copies ran while one was open for 1% of the time, Pallas kernels for 0%

profile of v1, /device:TPU:0, one launch (start us, length us, event | category | flops | bytes accessed | tf_op | source)
XLA Modules:
  0.0 797.5 jit_solution(8642645024768589274)
XLA Ops:
  7.2 0.0 all-gather.2.cloned.1.call-start
  7.2 0.7 all-gather.2.cloned.1.call-update
  7.9 0.0 reduce-scatter.2.cloned.1.call-start
  7.9 1.4 stack.2
  9.4 79.5 %all_to_all.5 = bf16[16,768,192]{1,2,0:T(8,128)(2,1)S(1)} all-to-all(bf16[16,768,192]{1,2,0:T(8,128)(2,1)S(1)} %stack.2), channel_id=1, replica_groups=mesh['blk'=16,'narrow'=8] {'blk'}, dimensions={0} | all-to-all | bytes 9437184 | tf_op jit(solution)/shard_map/all_to_all | solution.py:20
  88.9 0.0 copy-start.1
  88.9 2.7 copy.7
  91.6 1.4 all-gather.2.cloned.1.call-done
  93.0 0.0 copy-done.1
  93.0 16.0 %multiply_convert_fusion = bf16[192,12288]{1,0:T(8,128)(2,1)} fusion(bf16[12288,192]{0,1:T(8,128)(2,1)} %all-gather.2.cloned.1.call-done, bf16[192,12288]{1,0:T(8,128)(2,1)} %param.3, bf16[12288,192]{0,1:T(8,128)(2,1)} %bitcast.10, bf16[192,192]{1,0:T(8,128)(2,1)S(1)} %copy-done.1), kind=kOutput, calls=%fused_computation.3 | convolution fusion | flops 1833283584 | bytes 18948096 | tf_op jit(solution)/shard_map/dot_general | solution.py:27
  109.0 0.0 copy-start
  109.0 5.3 fusion.2
  114.4 0.0 copy-done
  114.4 6.4 convolution_multiply_fusion
  120.8 0.0 reduce-scatter.2.cloned.1.call-update
  120.8 669.8 %reduce-scatter.2.cloned.1.call-done = f32[96,192]{1,0:T(8,128)} async-done(((f32[12288,192]{1,0:T(8,128)}), f32[96,192]{1,0:T(8,128)}) %reduce-scatter.2.cloned.1.call-update) | async-done | bytes 73744 | tf_op jit(solution)/shard_map/reduce_scatter | solution.py:38
Async XLA Ops:
  7.2 85.9 %all-gather.2.cloned.1.call-start = ((), (), s32[]{:S(2)}) async-start(), calls=%async_computation.2 | async-start | bytes 5013504 | tf_op jit(solution)/shard_map/all_gather | solution.py:25
  7.9 782.8 %reduce-scatter.2.cloned.1.call-start = ((), (), s32[]{:S(2)}) async-start(), calls=%async_computation.3 | async-start | bytes 12681216 | tf_op jit(solution)/shard_map/reduce_scatter | solution.py:38
  88.9 4.1 copy-start.1
  109.0 5.3 copy-start
Sparse Core Ops, SparseCore 0:
  9.6 83.3 all-gather.1
  120.9 669.6 reduce-scatter.1
